TPU v7x, 32 devices: a whole 2x2x4 slice. The times are simulated.
32 devices in a mesh: wave: 16 (over z, x, core), level: 2 (over y).
Axes of the slice: x: 2, y: 2, z: 4, core: 2. Of those that a mesh axis runs over, the one named last changes fastest.
Arguments:
- state: float32 [4, 64, 256, 2, 256], P(None, 'level', 'wave'), may hold values from -0.02 to 0.02
- legendre: float32 [256, 384, 256], P('wave'), may hold values from -6 to 6
- lat_weight: float32 [384], P('wave'), may hold values from 0.8 to 2
- modes: float32 [64, 64], replicated, may hold values from -1 to 1, as said below
- mode_rates: float32 [64], replicated, may hold values from 1e-05 to 0.003
- diffusion: float32 [4], replicated, may hold values from 0.3 to 3
- norm_gain: float32 [256], replicated, may hold values from 0.5 to 1.5
- w_first: bfloat16 [1024, 256], replicated, may hold values from -0.375 to 0.375
- b_first: float32 [1024], replicated, may hold values from -3 to 3
- w_second: bfloat16 [1024, 1024], replicated, may hold values from -0.1875 to 0.1875
- b_second: float32 [1024], replicated, may hold values from -3 to 3
- w_third: bfloat16 [256, 1024], replicated, may hold values from -0.1875 to 0.1875
- b_third: float32 [256], replicated, may hold values from -1.2 to 1.2
Outputs:
- next_state: float32 [4, 64, 256, 2, 256], P(None, 'level', 'wave')
Inputs may be any that keep to these rules, and one draw needn't show every extreme that they name: `modes`: orthogonal: its transpose is its inverse.
All inputs are finite; a program needn't handle non-finite values.
Results may differ from a plain program's by a relative error of at most 0.0011.
Values may be sent and summed in bfloat16 or wider, within the bound.
A program may use at most 192 MiB of HBM per device.

v0:
```python
import jax
import jax.numpy as jnp
from jax import lax
from jax.sharding import PartitionSpec as P

M = 256
LAT = 384
LON = 768
highest = lax.Precision.HIGHEST
norm_eps = 1e-06


def phase_angles(waves, longitudes):
    wave_idx = jnp.arange(waves, dtype=jnp.int32)
    lon_idx = jnp.arange(longitudes, dtype=jnp.int32)
    phase_turns = wave_idx[:, None] * lon_idx[None, :] % longitudes
    return (2.0 * jnp.pi / longitudes * phase_turns.astype(jnp.float32), wave_idx)


def synthesis_table(waves, longitudes):
    angle_table, wave_idx = phase_angles(waves, longitudes)
    factor = jnp.where(wave_idx == 0, 1.0, 2.0).astype(jnp.float32)[:, None]
    return jnp.stack([factor * jnp.cos(angle_table), -factor * jnp.sin(angle_table)], axis=1)


def analysis_table(waves, longitudes):
    angle_table, wave_idx = phase_angles(waves, longitudes)
    flipped = angle_table.T
    return jnp.stack([jnp.cos(flipped), -jnp.sin(flipped)], axis=2) / longitudes


def column_physics(columns, norm_gain, w_first, b_first, w_second, b_second, w_third, b_third):
    values = columns.astype(jnp.float32)
    inverse_rms = lax.rsqrt(jnp.mean(values * values, axis=0, keepdims=True) + norm_eps)
    normed = (values * inverse_rms * norm_gain[:, None]).astype(jnp.bfloat16)
    hidden_one = jax.nn.gelu(
        jnp.dot(w_first, normed, preferred_element_type=jnp.float32) + b_first[:, None]
    ).astype(jnp.bfloat16)
    hidden_two = jax.nn.gelu(
        jnp.dot(w_second, hidden_one, preferred_element_type=jnp.float32) + b_second[:, None]
    ).astype(jnp.bfloat16)
    return (
        jnp.dot(w_third, hidden_two, preferred_element_type=jnp.float32) + b_third[:, None]
    ).astype(jnp.bfloat16)


def body(
    state,
    legendre,
    lat_weight,
    modes,
    mode_rates,
    diffusion,
    norm_gain,
    w_first,
    b_first,
    w_second,
    b_second,
    w_third,
    b_third,
):
    fields = state.shape[0]
    lev_dev = state.shape[1]
    m_dev = state.shape[2]
    complex_parts = state.shape[3]
    degrees = state.shape[4]
    levels = modes.shape[0]
    wave_count = lax.axis_size("wave")
    lat_dev = LAT // wave_count
    wave_global = lax.axis_index("wave") * m_dev + jnp.arange(m_dev, dtype=jnp.int32)
    degree_index = wave_global[:, None] + jnp.arange(degrees, dtype=jnp.int32)[None, :]
    kept_mask = (degree_index < M).astype(jnp.float32)
    kept_basis = legendre * kept_mask[:, None, :]
    basis_blocks = kept_basis.reshape(m_dev, wave_count, lat_dev, degrees)
    inverse_tab = synthesis_table(M, LON).reshape(wave_count, m_dev, complex_parts, LON)
    forward_tab = analysis_table(M, LON).reshape(LON, wave_count, m_dev, complex_parts)
    pieces = []
    for field_index in range(fields):
        band_coeffs = jnp.einsum(
            "lmcj,mwaj->wlcma", state[field_index], basis_blocks, precision=highest
        )
        exchanged = lax.all_to_all(
            band_coeffs.reshape(wave_count, -1), "wave", split_axis=0, concat_axis=0, tiled=True
        )
        shaped = exchanged.reshape(wave_count, lev_dev, complex_parts, m_dev, lat_dev)
        pieces.append(jnp.einsum("wlcma,wmco->lao", shaped, inverse_tab, precision=highest))
    grid_field = jnp.stack(pieces)
    grid_low = grid_field.astype(jnp.bfloat16)
    slab = grid_low.reshape(fields, lev_dev, lat_dev * LON)
    columns = lax.all_to_all(slab, "level", split_axis=2, concat_axis=1, tiled=True)
    col_count = columns.shape[2]
    tendency = column_physics(
        columns.reshape(fields * levels, col_count),
        norm_gain,
        w_first,
        b_first,
        w_second,
        b_second,
        w_third,
        b_third,
    )
    tendency = tendency.reshape(fields, levels, col_count)
    returned = lax.all_to_all(tendency, "level", split_axis=1, concat_axis=2, tiled=True).reshape(
        fields, lev_dev, lat_dev, LON
    )
    updated = (grid_field + returned.astype(jnp.float32)) * lat_weight[None, None, :, None]
    field_parts = []
    for field_index in range(fields):
        wave_coeffs = jnp.einsum(
            "lao,owmc->wlcma", updated[field_index], forward_tab, precision=highest
        )
        exchanged = lax.all_to_all(
            wave_coeffs.reshape(wave_count, -1), "wave", split_axis=0, concat_axis=0, tiled=True
        )
        shaped = exchanged.reshape(wave_count, lev_dev, complex_parts, m_dev, lat_dev)
        field_parts.append(jnp.einsum("wlcma,mwaj->lmcj", shaped, basis_blocks, precision=highest))
    spectral = jnp.stack(field_parts)
    growth = (degree_index * (degree_index + 1)).astype(jnp.float32)
    divisor = 1.0 + mode_rates[:, None, None, None] * growth[None, :, None, :]
    divisor = jnp.broadcast_to(divisor, (levels, m_dev, complex_parts, degrees)).reshape(levels, -1)
    divergence = spectral[1].reshape(lev_dev, -1)
    lev_start = lax.axis_index("level") * lev_dev
    own_rows = lax.dynamic_slice_in_dim(modes, lev_start, lev_dev, 0)
    amplitude = jnp.dot(
        modes.T,
        lax.all_gather(divergence, "level", axis=0, tiled=True),
        precision=highest,
        preferred_element_type=jnp.float32,
    )
    amplitude = amplitude / divisor
    solved = jnp.dot(own_rows, amplitude, precision=highest, preferred_element_type=jnp.float32)
    solved = solved.reshape(lev_dev, m_dev, complex_parts, degrees)
    combined = jnp.concatenate([spectral[:1], solved[None], spectral[2:]], axis=0)
    scaled_growth = growth / (M * (M - 1))
    damping = 1.0 + diffusion[:, None, None] * (scaled_growth * scaled_growth)[None]
    return combined / damping[:, None, :, None, :]


def solution(mesh):
    in_specs = (
        P(None, "level", "wave", None, None),
        P("wave", None, None),
        P("wave"),
        P(),
        P(),
        P(),
        P(),
        P(),
        P(),
        P(),
        P(),
        P(),
        P(),
    )
    out_specs = P(None, "level", "wave", None, None)
    return jax.shard_map(body, mesh=mesh, in_specs=in_specs, out_specs=out_specs, check_vma=False)
```

profile of v0, /device:TPU:0, one launch (start us, length us, event | category | flops | bytes accessed | tf_op | source)
XLA Modules:
  0.0 1027.8 jit_solution(9725989835272598431)
XLA Ops:
  24.2 10.3 %copy.193 = f32[16,32,2,16,24]{4,3,2,1,0:T(8,128)} copy(f32[16,32,2,16,24]{1,4,2,0,3:T(8,128)} %convolution_bitcast_fusion.8) | data formatting | bytes 3145728 | tf_op jit(solution)/shard_map/lmcj,mwaj->wlcma/transpose | solution.py:79
  34.5 9.1 all_to_all.80
  51.3 9.9 convolution_bitcast_fusion.7
  61.1 10.3 %copy.196 = f32[16,32,2,16,24]{4,3,2,1,0:T(8,128)} copy(f32[16,32,2,16,24]{1,4,2,0,3:T(8,128)} %convolution_bitcast_fusion.7) | data formatting | bytes 3145728 | tf_op jit(solution)/shard_map/lmcj,mwaj->wlcma/transpose | solution.py:79
  71.4 9.1 all_to_all.81
  92.3 9.9 convolution_bitcast_fusion.6
  102.2 10.3 %copy.199 = f32[16,32,2,16,24]{4,3,2,1,0:T(8,128)} copy(f32[16,32,2,16,24]{1,4,2,0,3:T(8,128)} %convolution_bitcast_fusion.6) | data formatting | bytes 3145728 | tf_op jit(solution)/shard_map/lmcj,mwaj->wlcma/transpose | solution.py:79
  112.5 9.2 all_to_all.82
  124.2 9.2 all-to-all-start.2
  133.4 12.3 %convolution_bitcast_fusion.5 = f32[16,32,2,16,24]{1,4,2,0,3:T(8,128)} fusion(f32[16,16,24,256,1]{3,2,4,1,0:T(8,128)} %bitcast.214, f32[1,32,16,2,256]{4,3,2,1,0:T(2,128)S(1)} %get-tuple-element.12), kind=kOutput, calls=%fused_computation.49 | convolution fusion | flops 1207959552 | bytes 8912896 | tf_op jit(solution)/shard_map/lmcj,mwaj->wlcma/dot_general | solution.py:79
  145.7 10.3 %copy.202 = f32[16,32,2,16,24]{4,3,2,1,0:T(8,128)} copy(f32[16,32,2,16,24]{1,4,2,0,3:T(8,128)} %convolution_bitcast_fusion.5) | data formatting | bytes 3145728 | tf_op jit(solution)/shard_map/lmcj,mwaj->wlcma/transpose | solution.py:79
  165.3 9.2 all-to-all-start.3
  185.7 9.2 reshape.350
  194.9 18.3 %bitcast_convert_fusion.3 = (bf16[32,24,768]{2,1,0:T(8,128)(2,1)}, f32[32,24,768,1,1]{2,1,3,0,4:T(8,128)}) fusion(f32[16,32,2,16,24]{4,3,2,1,0:T(8,128)} %reshape.350, f32[16,16,1,768]{3,1,2,0:T(8,128)} %get-tuple-element.16, f32[16,16,1,768]{3,1,2,0:T(8,128)S(1)} %get-tuple-element.15), kind=kOutput, calls=%fused_computation.64 | convolution fusion | flops 3624861696 | bytes 6684672 | tf_op jit(solution)/shard_map/wlcma,wmco->lao/dot_general | solution.py:86
  222.0 9.4 reshape.351
  231.4 17.9 %bitcast_convert_fusion.2 = (bf16[32,24,768]{2,1,0:T(8,128)(2,1)}, f32[32,24,768,1,1]{2,1,3,0,4:T(8,128)}) fusion(f32[16,32,2,16,24]{4,3,2,1,0:T(8,128)} %reshape.351, f32[16,16,1,768]{3,1,2,0:T(8,128)} %get-tuple-element.16, f32[16,16,1,768]{3,1,2,0:T(8,128)S(1)} %get-tuple-element.15), kind=kOutput, calls=%fused_computation.63 | convolution fusion | flops 3624861696 | bytes 6684672 | tf_op jit(solution)/shard_map/wlcma,wmco->lao/dot_general | solution.py:86
  258.2 9.2 reshape.352
  267.5 17.8 %bitcast_convert_fusion.1 = (bf16[32,24,768]{2,1,0:T(8,128)(2,1)}, f32[32,24,768,1,1]{2,1,3,0,4:T(8,128)}) fusion(f32[16,32,2,16,24]{4,3,2,1,0:T(8,128)} %reshape.352, f32[16,16,1,768]{3,1,2,0:T(8,128)} %get-tuple-element.16, f32[16,16,1,768]{3,1,2,0:T(8,128)S(1)} %get-tuple-element.15), kind=kOutput, calls=%fused_computation.62 | convolution fusion | flops 3624861696 | bytes 6684672 | tf_op jit(solution)/shard_map/wlcma,wmco->lao/dot_general | solution.py:86
  294.5 9.2 reshape.353
  303.7 17.8 %bitcast_convert_fusion = (bf16[32,24,768]{2,1,0:T(8,128)(2,1)}, f32[32,24,768,1,1]{2,1,3,0,4:T(8,128)}) fusion(f32[16,32,2,16,24]{4,3,2,1,0:T(8,128)} %reshape.353, f32[16,16,1,768]{3,1,2,0:T(8,128)} %get-tuple-element.16, f32[16,16,1,768]{3,1,2,0:T(8,128)S(1)} %get-tuple-element.15), kind=kOutput, calls=%fused_computation.61 | convolution fusion | flops 3624861696 | bytes 6684672 | tf_op jit(solution)/shard_map/wlcma,wmco->lao/dot_general | solution.py:86
  327.0 22.5 %copy.204 = bf16[4,32,18432]{1,0,2:T(4,128)(2,1)} copy(bf16[4,32,18432]{2,1,0:T(8,128)(2,1)} %pad_maximum_fusion) | data formatting | bytes 9437184 | tf_op jit(solution)/shard_map/stack | solution.py:87
  349.5 27.9 %reshape.391 = bf16[2,2,589824]{2,1,0:T(2,128)(2,1)} reshape(bf16[18432,4,32]{2,1,0:T(4,128)(2,1)} %bitcast.221) | data formatting | bytes 9437184
  377.5 61.9 %all_to_all.98 = bf16[2,2,589824]{2,1,0:T(2,128)(2,1)} all-to-all(bf16[2,2,589824]{2,1,0:T(2,128)(2,1)} %reshape.391), channel_id=1, replica_groups=mesh['wave'=16,'level'=2] {'level'}, dimensions={0} | all-to-all | bytes 9437184 | tf_op jit(solution)/shard_map/all_to_all | solution.py:90
  439.4 20.3 %reshape.392 = bf16[18432,4,32]{2,1,0:T(4,128)(2,1)} reshape(bf16[2,2,589824]{2,1,0:T(2,128)(2,1)} %all_to_all.98) | data formatting | bytes 9437184
  459.7 22.8 %copy.205 = bf16[4,32,18432]{2,1,0:T(8,128)(2,1)} copy(bf16[4,32,18432]{1,0,2:T(4,128)(2,1)} %bitcast.222) | data formatting | bytes 9437184 | tf_op jit(solution)/shard_map/all_to_all | solution.py:90
  482.5 12.7 %reshape.362 = f32[4,32,2,9216]{3,2,1,0:T(2,128)} reshape(bf16[4,32,18432]{2,1,0:T(8,128)(2,1)} %copy.205) | data formatting | bytes 14155776 | tf_op jit(solution)/shard_map/convert_element_type | solution.py:33
  498.6 10.2 copy.206
  513.9 19.4 %fusion.7.clone.4 = bf16[1024,9216]{0,1:T(8,128)(2,1)} fusion(bf16[256,9216]{1,0:T(8,128)(2,1)S(1)} %fusion.24, bf16[1024,256]{1,0:T(8,128)(2,1)S(1)} %copy-done.17, f32[1024]{0:T(1024)S(1)} %copy-done.19), kind=kOutput, calls=%fused_computation.9.clone.clone.clone.1 | convolution fusion | flops 4926210048 | bytes 24121344 | tf_op jit(solution)/shard_map/dot_general | solution.py:37
  533.4 38.6 %fusion.15 = bf16[1024,9216]{0,1:T(8,128)(2,1)} fusion(bf16[1024,1024]{1,0:T(8,128)(2,1)S(1)} %copy-done, f32[1024]{0:T(1024)S(1)} %copy-done.20, bf16[1024,9216]{0,1:T(8,128)(2,1)} %fusion.7.clone.4), kind=kOutput, calls=%fused_computation.17 | convolution fusion | flops 19421724672 | bytes 39849984 | tf_op jit(solution)/shard_map/dot_general | solution.py:40
  571.9 19.2 %fusion.21 = bf16[9216,256]{0,1:T(8,128)(2,1)S(1)} fusion(bf16[1024,9216]{0,1:T(8,128)(2,1)} %fusion.15, bf16[256,1024]{1,0:T(8,128)(2,1)S(1)} %copy-done.18, f32[256]{0:T(256)S(1)} %copy-done.21), kind=kOutput, calls=%fused_computation.24 | convolution fusion | flops 4836556800 | bytes 24118272 | tf_op jit(solution)/shard_map/dot_general | solution.py:43
  606.2 49.7 %all-to-all-done.5 = bf16[4,64,9216]{2,0,1:T(4,128)(2,1)} async-done(((bf16[4,64,9216]{2,0,1:T(4,128)(2,1)}), bf16[4,64,9216]{2,0,1:T(4,128)(2,1)}, u32[]{:S(2)}, u32[]{:S(2)}) %all-to-all-start.5) | async-done | bytes 4718624 | tf_op jit(solution)/shard_map/all_to_all | solution.py:103
  669.1 13.1 %reshape.361 = f32[4,32,24,768]{3,2,1,0:T(8,128)} reshape(f32[4,32,2,9216]{3,2,1,0:T(2,128)} %copy.209) | data formatting | bytes 18874368 | tf_op jit(solution)/shard_map/convert_element_type | solution.py:106
  692.5 17.0 %convolution_bitcast_fusion.3 = f32[16,32,2,16,24]{1,3,4,2,0:T(8,128)} fusion(f32[32,24,768,1,1]{2,1,0,4,3:T(8,128)S(1)} %get-tuple-element.8, f32[768,16,16,1]{0,2,3,1:T(8,128)S(1)} %get-tuple-element.14, f32[768,16,16,1]{0,2,3,1:T(8,128)S(1)} %get-tuple-element.13), kind=kOutput, calls=%fused_computation.47 | convolution fusion | flops 3624665088 | bytes 5505024 | tf_op jit(solution)/shard_map/lao,owmc->wlcma/dot_general | solution.py:109
  709.4 10.6 %copy.215 = f32[16,32,2,16,24]{4,3,2,1,0:T(8,128)} copy(f32[16,32,2,16,24]{1,3,4,2,0:T(8,128)} %convolution_bitcast_fusion.3) | data formatting | bytes 3145728 | tf_op jit(solution)/shard_map/lao,owmc->wlcma/transpose | solution.py:109
  720.1 9.2 all_to_all.85
  734.7 18.4 %convolution_bitcast_fusion.4 = f32[16,32,2,16,24]{1,3,4,2,0:T(8,128)} fusion(f32[32,24,768,1,1]{2,1,0,4,3:T(8,128)} %get-tuple-element.5, f32[768,16,16,1]{0,2,3,1:T(8,128)} %copy-done.7, f32[768,16,16,1]{0,2,3,1:T(8,128)S(1)} %get-tuple-element.13), kind=kOutput, calls=%fused_computation.48 | convolution fusion | flops 3624665088 | bytes 5505024 | tf_op jit(solution)/shard_map/lao,owmc->wlcma/dot_general | solution.py:109
  753.1 10.5 %copy.211 = f32[16,32,2,16,24]{4,3,2,1,0:T(8,128)} copy(f32[16,32,2,16,24]{1,3,4,2,0:T(8,128)} %convolution_bitcast_fusion.4) | data formatting | bytes 3145728 | tf_op jit(solution)/shard_map/lao,owmc->wlcma/transpose | solution.py:109
  763.6 9.1 all_to_all.84
  780.1 18.4 %convolution_bitcast_fusion.2 = f32[16,32,2,16,24]{1,3,4,2,0:T(8,128)} fusion(f32[32,24,768,1,1]{2,1,0,4,3:T(8,128)} %get-tuple-element.7, f32[768,16,16,1]{0,2,3,1:T(8,128)} %copy-done.7, f32[768,16,16,1]{0,2,3,1:T(8,128)S(1)} %get-tuple-element.13), kind=kOutput, calls=%fused_computation.46 | convolution fusion | flops 3624665088 | bytes 5505024 | tf_op jit(solution)/shard_map/lao,owmc->wlcma/dot_general | solution.py:109
  798.6 10.5 %copy.220 = f32[16,32,2,16,24]{4,3,2,1,0:T(8,128)} copy(f32[16,32,2,16,24]{1,3,4,2,0:T(8,128)} %convolution_bitcast_fusion.2) | data formatting | bytes 3145728 | tf_op jit(solution)/shard_map/lao,owmc->wlcma/transpose | solution.py:109
  809.1 9.1 all_to_all.86
  824.8 18.4 %convolution_bitcast_fusion.1 = f32[16,32,2,16,24]{1,3,4,2,0:T(8,128)} fusion(f32[32,24,768,1,1]{2,1,0,4,3:T(8,128)} %get-tuple-element.6, f32[768,16,16,1]{0,2,3,1:T(8,128)} %copy-done.7, f32[768,16,16,1]{0,2,3,1:T(8,128)S(1)} %get-tuple-element.13), kind=kOutput, calls=%fused_computation.45 | convolution fusion | flops 3624665088 | bytes 5505024 | tf_op jit(solution)/shard_map/lao,owmc->wlcma/dot_general | solution.py:109
  843.2 10.5 %copy.224 = f32[16,32,2,16,24]{4,3,2,1,0:T(8,128)} copy(f32[16,32,2,16,24]{1,3,4,2,0:T(8,128)} %convolution_bitcast_fusion.1) | data formatting | bytes 3145728 | tf_op jit(solution)/shard_map/lao,owmc->wlcma/transpose | solution.py:109
  853.7 9.1 all_to_all.87
  882.9 18.7 %fusion.42 = f32[32,16,2,256]{3,0,2,1:T(8,128)S(1)} fusion(f32[16,16,24,256,1]{3,2,1,4,0:T(8,128)} %bitcast.215, f32[16,32,2,16,24]{4,3,2,1,0:T(8,128)} %reshape.356), kind=kOutput, calls=%fused_computation.69 | convolution fusion | flops 1207959552 | bytes 8912896 | tf_op jit(solution)/shard_map/wlcma,mwaj->lmcj/dot_general | solution.py:116
  948.3 18.6 %fusion.39 = f32[1,32,16,2,256]{4,1,3,2,0:T(8,128)S(1)} fusion(f32[16,16,24,256,1]{3,2,1,4,0:T(8,128)} %bitcast.216, f32[16,32,2,16,24]{4,3,2,1,0:T(8,128)} %reshape.355), kind=kOutput, calls=%fused_computation.68 | convolution fusion | flops 1207959552 | bytes 8912896 | tf_op jit(solution)/shard_map/wlcma,mwaj->lmcj/dot_general | solution.py:116
  966.9 20.0 %fusion.45 = f32[1,32,16,2,256]{4,1,3,2,0:T(8,128)} fusion(f32[16,16,24,256,1]{3,2,1,4,0:T(8,128)} %bitcast.217, f32[16,32,2,16,24]{4,3,2,1,0:T(8,128)} %reshape.358), kind=kOutput, calls=%fused_computation.70 | convolution fusion | flops 1207959552 | bytes 8912896 | tf_op jit(solution)/shard_map/wlcma,mwaj->lmcj/dot_general | solution.py:116
  987.0 19.6 %fusion.48 = f32[1,32,16,2,256]{4,1,3,2,0:T(8,128)} fusion(f32[16,16,24,256,1]{3,2,1,4,0:T(8,128)S(1)} %bitcast.220, f32[16,32,2,16,24]{4,3,2,1,0:T(8,128)S(1)} %bitcast.224), kind=kOutput, calls=%fused_computation.71 | convolution fusion | flops 1207959552 | bytes 8912896 | tf_op jit(solution)/shard_map/wlcma,mwaj->lmcj/dot_general | solution.py:116
  (124 shorter events, 239.6 us)
Async XLA Ops:
  6.5 526.8 %copy-start = (bf16[1024,1024]{1,0:T(8,128)(2,1)S(1)}, bf16[1024,1024]{1,0:T(8,128)(2,1)}, u32[]{:S(2)}) copy-start(bf16[1024,1024]{1,0:T(8,128)(2,1)} %param.22) | copy-start | bytes 6291460
  6.5 6.9 copy-start.3
  6.5 0.5 copy-start.11
  14.0 2.6 copy-start.2
  43.7 39.5 %all-to-all-start = ((f32[16,1,24576]{2,1,0:T(1,128)}), f32[16,1,24576]{2,1,0:T(1,128)}, u32[]{:S(2)}, u32[]{:S(2)}) async-start(f32[16,1,24576]{2,1,0:T(1,128)} %all_to_all.80), calls=%async_computation | async-start | bytes 3145728 | tf_op jit(solution)/shard_map/all_to_all | solution.py:82
  83.2 41.0 %all-to-all-start.1 = ((f32[16,1,24576]{2,1,0:T(1,128)}), f32[16,1,24576]{2,1,0:T(1,128)}, u32[]{:S(2)}, u32[]{:S(2)}) async-start(f32[16,1,24576]{2,1,0:T(1,128)} %all_to_all.81), calls=%async_computation.1 | async-start | bytes 3145728 | tf_op jit(solution)/shard_map/all_to_all | solution.py:82
  124.2 41.1 %all-to-all-start.2 = ((f32[16,1,24576]{2,1,0:T(1,128)}), f32[16,1,24576]{2,1,0:T(1,128)}, u32[]{:S(2)}, u32[]{:S(2)}) async-start(f32[16,1,24576]{2,1,0:T(1,128)} %all_to_all.82), calls=%async_computation.2 | async-start | bytes 3145728 | tf_op jit(solution)/shard_map/all_to_all | solution.py:82
  165.3 122.8 %all-to-all-start.3 = ((f32[16,1,24576]{2,1,0:T(1,128)}), f32[16,1,24576]{2,1,0:T(1,128)}, u32[]{:S(2)}, u32[]{:S(2)}) async-start(f32[16,1,24576]{2,1,0:T(1,128)} %all_to_all.83), calls=%async_computation.3 | async-start | bytes 3145728 | tf_op jit(solution)/shard_map/all_to_all | solution.py:82
  174.5 0.6 copy-start.8
  498.6 10.4 %copy-start.13 = (f32[256]{0:T(256)S(1)}, f32[256]{0:T(256)}, u32[]{:S(2)}) copy-start(f32[256]{0:T(256)} %param.19) | copy-start | bytes 3076
  508.9 5.0 copy-start.17
  508.9 5.0 copy-start.19
  513.9 19.4 %copy-start.20 = (f32[1024]{0:T(1024)S(1)}, f32[1024]{0:T(1024)}, u32[]{:S(2)}) copy-start(f32[1024]{0:T(1024)} %param.23) | copy-start | bytes 12292
  533.4 38.6 %copy-start.18 = (bf16[256,1024]{1,0:T(8,128)(2,1)S(1)}, bf16[256,1024]{1,0:T(8,128)(2,1)}, u32[]{:S(2)}) copy-start(bf16[256,1024]{1,0:T(8,128)(2,1)} %param.24) | copy-start | bytes 1572868
  533.4 38.6 %copy-start.21 = (f32[256]{0:T(256)S(1)}, f32[256]{0:T(256)}, u32[]{:S(2)}) copy-start(f32[256]{0:T(256)} %param.25) | copy-start | bytes 3076
  597.0 5.9 copy-start.9
  597.0 58.9 %all-to-all-start.5 = ((bf16[4,64,9216]{2,0,1:T(4,128)(2,1)}), bf16[4,64,9216]{2,0,1:T(4,128)(2,1)}, u32[]{:S(2)}, u32[]{:S(2)}) async-start(bf16[4,64,9216]{2,0,1:T(4,128)(2,1)} %copy.207), calls=%async_computation.5 | async-start | bytes 9437184 | tf_op jit(solution)/shard_map/all_to_all | solution.py:103
  606.2 86.3 %copy-start.7 = (f32[768,16,16,1]{0,2,3,1:T(8,128)}, f32[768,16,16,1]{0,2,3,1:T(8,128)S(1)}, u32[]{:S(2)}) copy-start(f32[768,16,16,1]{0,2,3,1:T(8,128)S(1)} %get-tuple-element.14) | copy-start | bytes 2359300
  669.1 13.1 %copy-start.16 = (f32[24]{0:T(128)S(1)}, f32[24]{0:T(128)}, u32[]{:S(2)}) copy-start(f32[24]{0:T(128)} %param.15) | copy-start | bytes 292
  729.2 43.5 %all-to-all-start.7 = ((f32[16,1,24576]{2,1,0:T(1,128)}), f32[16,1,24576]{2,1,0:T(1,128)S(1)}, u32[]{:S(2)}, u32[]{:S(2)}) async-start(f32[16,1,24576]{2,1,0:T(1,128)} %all_to_all.85), calls=%async_computation.7 | async-start | bytes 3145728 | tf_op jit(solution)/shard_map/all_to_all | solution.py:112
  772.8 1.1 copy-start.5
  773.9 44.3 %all-to-all-start.6 = ((f32[16,1,24576]{2,1,0:T(1,128)}), f32[16,1,24576]{2,1,0:T(1,128)S(1)}, u32[]{:S(2)}, u32[]{:S(2)}) async-start(f32[16,1,24576]{2,1,0:T(1,128)} %all_to_all.84), calls=%async_computation.6 | async-start | bytes 3145728 | tf_op jit(solution)/shard_map/all_to_all | solution.py:112
  818.2 25.0 %copy-start.4 = (f32[16,1,24576]{2,1,0:T(1,128)}, f32[16,1,24576]{2,1,0:T(1,128)S(1)}, u32[]{:S(2)}) copy-start(f32[16,1,24576]{2,1,0:T(1,128)S(1)} %all-to-all-done.6) | copy-start | bytes 4718596
  818.2 44.7 %all-to-all-start.8 = ((f32[16,1,24576]{2,1,0:T(1,128)}), f32[16,1,24576]{2,1,0:T(1,128)}, u32[]{:S(2)}, u32[]{:S(2)}) async-start(f32[16,1,24576]{2,1,0:T(1,128)} %all_to_all.86), calls=%async_computation.8 | async-start | bytes 3145728 | tf_op jit(solution)/shard_map/all_to_all | solution.py:112
  853.7 15.4 %copy-start.12 = (s32[16]{0:T(128)S(1)}, s32[16]{0:T(128)}, u32[]{:S(2)}) copy-start(s32[16]{0:T(128)} %copy-done.11) | copy-start | bytes 196
  853.7 15.5 %copy-start.14 = (f32[64]{0:T(128)S(1)}, f32[64]{0:T(128)}, u32[]{:S(2)}) copy-start(f32[64]{0:T(128)} %param.17) | copy-start | bytes 772
  862.9 71.9 %all-to-all-start.9 = ((f32[16,1,24576]{2,1,0:T(1,128)}), f32[16,1,24576]{2,1,0:T(1,128)}, u32[]{:S(2)}, u32[]{:S(2)}) async-start(f32[16,1,24576]{2,1,0:T(1,128)} %all_to_all.87), calls=%async_computation.9 | async-start | bytes 3145728 | tf_op jit(solution)/shard_map/all_to_all | solution.py:112
  869.0 137.6 %all-gather.2.cloned.1.call-start = ((), (), s32[]{:S(2)}) async-start(), calls=%async_computation.10 | async-start | bytes 3145728 | tf_op jit(solution)/shard_map/all_gather | solution.py:126
  901.6 2.8 copy-start.15
  948.3 38.7 %slice-start = ((s8[6291456]{0:T(1024)(128)(4,1)}), s8[4194304]{0:T(1024)(128)(4,1)S(1)}, s32[]{:S(2)}) async-start(s8[6291456]{0:T(1024)(128)(4,1)} %bitcast.218), calls=%async_computation.11 | async-start | bytes 8388608
  948.3 38.7 %slice-start.2 = ((s8[8388608]{0:T(1024)(128)(4,1)}), s8[4194304]{0:T(1024)(128)(4,1)S(1)}, s32[]{:S(2)}) async-start(s8[8388608]{0:T(1024)(128)(4,1)} %bitcast.223), calls=%async_computation.13 | async-start | bytes 8388608
  966.9 20.1 %slice-start.1 = ((s8[6291456]{0:T(1024)(128)(4,1)}), s8[2097152]{0:T(1024)(128)(4,1)S(1)}, s32[]{:S(2)}) async-start(s8[6291456]{0:T(1024)(128)(4,1)} %bitcast.218), calls=%async_computation.12 | async-start | bytes 4194304
  966.9 20.1 %slice-start.3 = ((s8[8388608]{0:T(1024)(128)(4,1)}), s8[4194304]{0:T(1024)(128)(4,1)S(1)}, s32[]{:S(2)}) async-start(s8[8388608]{0:T(1024)(128)(4,1)} %bitcast.223), calls=%async_computation.14 | async-start | bytes 8388608
  987.0 19.6 %copy-start.6 = (f32[64,8192]{1,0:T(8,128)S(1)}, f32[64,8192]{1,0:T(8,128)}, u32[]{:S(2)}) copy-start(f32[64,8192]{1,0:T(8,128)} %reshape.357) | copy-start | bytes 6291460
  987.0 19.6 %copy-start.10 = (f32[64,64]{1,0:T(8,128)S(1)}, f32[64,64]{1,0:T(8,128)}, u32[]{:S(2)}) copy-start(f32[64,64]{1,0:T(8,128)} %param.16) | copy-start | bytes 49156
  1012.9 7.8 copy-start.1
Sparse Core Ops, SparseCore 0:
  904.5 33.4 all-gather.1
where the time goes:
time: 1040 us; the launch traced here: 1030 us
  local copies, waits for them, and re-layouts  411 us (40%)
  matrix products  343 us (33%)
  other arithmetic  77.7 us (7%)
  starting transfers between devices  65.4 us (6%)
  blocking collectives  61.9 us (6%)
  waiting for transfers between devices  55 us (5%)
  between operations  14.2 us (1%)
    dot_general x4, matrix products, body(): jnp.einsum('wlcma,mwaj->lmcj', shaped, basis_blocks, precision=highest)  76.9 us
    dot_general x4, matrix products, body(): jnp.einsum('lao,owmc->wlcma', updated[field_index], forward_tab, precisio...  72.3 us
    dot_general x4, matrix products, body(): jnp.einsum('wlcma,wmco->lao', shaped, inverse_tab, precision=highest)  71.8 us
    reshape x8, local copies, waits for them, and re-layouts, body(): exchanged.reshape(wave_count, lev_dev, complex_parts, m_dev, lat_dev)  70.1 us
    all_to_all x1, blocking collectives, body(): lax.all_to_all(slab, 'level', split_axis=2, concat_axis=1, tiled=True)  61.9 us
    unnamed x54, local copies, waits for them, and re-layouts  53.2 us
    all_to_all x1, waiting for transfers between devices, body(): lax.all_to_all(tendency, 'level', split_axis=1, concat_axis=2, tiled=True)  49.7 us
    transpose x4, local copies, waits for them, and re-layouts, body(): jnp.einsum('lao,owmc->wlcma', updated[field_index], forward_tab, precisio...  42.1 us
  transfers between devices with their start and end apart: 10, of which 4 were waited for; matrix products, arithmetic and copies ran while one was open for 39% of the time, Pallas kernels for 0%

commit v1 on v0

--- a/solution.py
+++ b/solution.py
@@ -87,7 +87,10 @@
     grid_field = jnp.stack(pieces)
     grid_low = grid_field.astype(jnp.bfloat16)
     slab = grid_low.reshape(fields, lev_dev, lat_dev * LON)
-    columns = lax.all_to_all(slab, "level", split_axis=2, concat_axis=1, tiled=True)
+    columns = jnp.concatenate(
+        lax.all_to_all(jnp.stack(jnp.split(slab, lax.axis_size("level"), axis=2)), "level", 0, 0),
+        axis=1,
+    )
     col_count = columns.shape[2]
     tendency = column_physics(
         columns.reshape(fields * levels, col_count),

time: 1040 us -> 916 us (0.88)
  local copies, waits for them, and re-layouts: 411 us -> 306 us
    unnamed x54 -> x59, local copies, waits for them, and re-layouts: 53.2 us -> 10.9 us
    convert_element_type x2 -> x0, local copies, waits for them, and re-layouts: 22.8 us -> none  [column_physics(): values = columns.astype(jnp.float32)]
    all_to_all x1 -> x0, local copies, waits for them, and re-layouts: 22.8 us -> none  [body(): lax.all_to_all(slab, 'level', split_axis=2, concat_axis=1, tiled=True)]
    another operation x5, local copies, waits for them, and re-layouts: 32.1 us -> 11.6 us  [body(): grid_field = jnp.stack(pieces)]
  transfers between devices with their start and end apart: 10 -> 10, of which waited for: 4 -> 3; matrix products, arithmetic and copies ran while one was open for 39% -> 45% of each run, Pallas kernels for 0% -> 0%
where the time goes in v1:
time: 916 us; the launch traced here: 906 us
  matrix products  342 us (37%)
  local copies, waits for them, and re-layouts  306 us (33%)
  other arithmetic  69.2 us (8%)
  starting transfers between devices  62.2 us (7%)
  blocking collectives  56.6 us (6%)
  waiting for transfers between devices  55.1 us (6%)
  between operations  14.4 us (2%)
    dot_general x4, matrix products, body(): jnp.einsum('wlcma,mwaj->lmcj', shaped, basis_blocks, precision=highest)  76.7 us
    dot_general x4, matrix products, body(): jnp.einsum('lao,owmc->wlcma', updated[field_index], forward_tab, precisio...  72.4 us
    dot_general x4, matrix products, body(): jnp.einsum('wlcma,wmco->lao', shaped, inverse_tab, precision=highest)  71.4 us
    reshape x8, local copies, waits for them, and re-layouts, body(): exchanged.reshape(wave_count, lev_dev, complex_parts, m_dev, lat_dev)  70.8 us
    all_to_all x1, blocking collectives, body(): lax.all_to_all(jnp.stack(jnp.split(slab, lax.axis_size('level'), axis=2))...  56.6 us
    all_to_all x1, waiting for transfers between devices, body(): lax.all_to_all(tendency, 'level', split_axis=1, concat_axis=2, tiled=True)  49.8 us
    transpose x4, local copies, waits for them, and re-layouts, body(): jnp.einsum('lao,owmc->wlcma', updated[field_index], forward_tab, precisio...  42.3 us
    transpose x4, local copies, waits for them, and re-layouts, body(): jnp.einsum('lmcj,mwaj->wlcma', state[field_index], basis_blocks, precisio...  41.2 us
  transfers between devices with their start and end apart: 10, of which 3 were waited for; matrix products, arithmetic and copies ran while one was open for 45% of the time, Pallas kernels for 0%

profile of v1, /device:TPU:0, one launch (start us, length us, event | category | flops | bytes accessed | tf_op | source)
XLA Modules:
  0.0 905.7 jit_solution(2805521089622789569)
XLA Ops:
  24.3 10.3 %copy.55 = f32[16,32,2,16,24]{4,3,2,1,0:T(8,128)} copy(f32[16,32,2,16,24]{1,4,2,0,3:T(8,128)} %convolution_bitcast_fusion.8) | data formatting | bytes 3145728 | tf_op jit(solution)/shard_map/lmcj,mwaj->wlcma/transpose | solution.py:79
  34.6 9.1 %all_to_all.76 = f32[16,1,24576]{2,1,0:T(1,128)} reshape(f32[16,32,2,16,24]{4,3,2,1,0:T(8,128)} %copy.55) | data formatting | bytes 3145728 | tf_op jit(solution)/shard_map/all_to_all | solution.py:82
  51.4 9.8 %convolution_bitcast_fusion.7 = f32[16,32,2,16,24]{1,4,2,0,3:T(8,128)} fusion(f32[16,16,24,256,1]{3,2,4,1,0:T(8,128)} %bitcast.215, f32[1,32,16,2,256]{4,3,2,1,0:T(2,128)} %get-tuple-element.13), kind=kOutput, calls=%fused_computation.52 | convolution fusion | flops 1207959552 | bytes 8912896 | tf_op jit(solution)/shard_map/lmcj,mwaj->wlcma/dot_general | solution.py:79
  61.2 10.3 %copy.58 = f32[16,32,2,16,24]{4,3,2,1,0:T(8,128)} copy(f32[16,32,2,16,24]{1,4,2,0,3:T(8,128)} %convolution_bitcast_fusion.7) | data formatting | bytes 3145728 | tf_op jit(solution)/shard_map/lmcj,mwaj->wlcma/transpose | solution.py:79
  71.5 9.1 %all_to_all.77 = f32[16,1,24576]{2,1,0:T(1,128)} reshape(f32[16,32,2,16,24]{4,3,2,1,0:T(8,128)} %copy.58) | data formatting | bytes 3145728 | tf_op jit(solution)/shard_map/all_to_all | solution.py:82
  83.3 9.1 %all-to-all-start.1 = ((f32[16,1,24576]{2,1,0:T(1,128)}), f32[16,1,24576]{2,1,0:T(1,128)}, u32[]{:S(2)}, u32[]{:S(2)}) async-start(f32[16,1,24576]{2,1,0:T(1,128)} %all_to_all.77), calls=%async_computation.1 | async-start | bytes 3145728 | tf_op jit(solution)/shard_map/all_to_all | solution.py:82
  92.4 9.8 %convolution_bitcast_fusion.6 = f32[16,32,2,16,24]{1,4,2,0,3:T(8,128)} fusion(f32[16,16,24,256,1]{3,2,4,1,0:T(8,128)} %bitcast.216, f32[1,32,16,2,256]{4,3,2,1,0:T(2,128)} %get-tuple-element.12), kind=kOutput, calls=%fused_computation.51 | convolution fusion | flops 1207959552 | bytes 8912896 | tf_op jit(solution)/shard_map/lmcj,mwaj->wlcma/dot_general | solution.py:79
  102.2 10.3 %copy.61 = f32[16,32,2,16,24]{4,3,2,1,0:T(8,128)} copy(f32[16,32,2,16,24]{1,4,2,0,3:T(8,128)} %convolution_bitcast_fusion.6) | data formatting | bytes 3145728 | tf_op jit(solution)/shard_map/lmcj,mwaj->wlcma/transpose | solution.py:79
  112.5 9.1 %all_to_all.78 = f32[16,1,24576]{2,1,0:T(1,128)} reshape(f32[16,32,2,16,24]{4,3,2,1,0:T(8,128)} %copy.61) | data formatting | bytes 3145728 | tf_op jit(solution)/shard_map/all_to_all | solution.py:82
  124.3 9.2 %all-to-all-start.2 = ((f32[16,1,24576]{2,1,0:T(1,128)}), f32[16,1,24576]{2,1,0:T(1,128)}, u32[]{:S(2)}, u32[]{:S(2)}) async-start(f32[16,1,24576]{2,1,0:T(1,128)} %all_to_all.78), calls=%async_computation.2 | async-start | bytes 3145728 | tf_op jit(solution)/shard_map/all_to_all | solution.py:82
  133.5 12.3 %convolution_bitcast_fusion.5 = f32[16,32,2,16,24]{1,4,2,0,3:T(8,128)} fusion(f32[16,16,24,256,1]{3,2,4,1,0:T(8,128)} %bitcast.217, f32[1,32,16,2,256]{4,3,2,1,0:T(2,128)S(1)} %get-tuple-element.11), kind=kOutput, calls=%fused_computation.50 | convolution fusion | flops 1207959552 | bytes 8912896 | tf_op jit(solution)/shard_map/lmcj,mwaj->wlcma/dot_general | solution.py:79
  145.8 10.3 %copy.64 = f32[16,32,2,16,24]{4,3,2,1,0:T(8,128)} copy(f32[16,32,2,16,24]{1,4,2,0,3:T(8,128)} %convolution_bitcast_fusion.5) | data formatting | bytes 3145728 | tf_op jit(solution)/shard_map/lmcj,mwaj->wlcma/transpose | solution.py:79
  156.1 9.1 %all_to_all.79 = f32[16,1,24576]{2,1,0:T(1,128)} reshape(f32[16,32,2,16,24]{4,3,2,1,0:T(8,128)} %copy.64) | data formatting | bytes 3145728 | tf_op jit(solution)/shard_map/all_to_all | solution.py:82
  176.5 9.4 %reshape.344 = f32[16,32,2,16,24]{4,3,2,1,0:T(8,128)} reshape(f32[16,24576]{1,0:T(8,128)} %reduce.2) | data formatting | bytes 3145728 | tf_op jit(solution)/shard_map/reshape | solution.py:85
  185.9 17.8 %bitcast_convert_fusion.3 = (bf16[32,24,768]{2,1,0:T(8,128)(2,1)}, f32[32,24,768,1,1]{2,1,3,0,4:T(8,128)}) fusion(f32[16,32,2,16,24]{4,3,2,1,0:T(8,128)} %reshape.344, f32[16,16,1,768]{3,1,2,0:T(8,128)} %get-tuple-element.18, f32[16,16,1,768]{3,1,2,0:T(8,128)S(1)} %get-tuple-element.17), kind=kOutput, calls=%fused_computation.67 | convolution fusion | flops 3624861696 | bytes 6684672 | tf_op jit(solution)/shard_map/wlcma,wmco->lao/dot_general | solution.py:86
  212.7 9.2 %reshape.345 = f32[16,32,2,16,24]{4,3,2,1,0:T(8,128)} reshape(f32[16,24576]{1,0:T(8,128)} %reduce.3) | data formatting | bytes 3145728 | tf_op jit(solution)/shard_map/reshape | solution.py:85
  228.2 17.8 %bitcast_convert_fusion.2 = (bf16[32,24,768]{2,1,0:T(8,128)(2,1)}, f32[32,24,768,1,1]{2,1,3,0,4:T(8,128)}) fusion(f32[16,32,2,16,24]{4,3,2,1,0:T(8,128)} %reshape.345, f32[16,16,1,768]{3,1,2,0:T(8,128)} %get-tuple-element.18, f32[16,16,1,768]{3,1,2,0:T(8,128)S(1)} %get-tuple-element.17), kind=kOutput, calls=%fused_computation.66 | convolution fusion | flops 3624861696 | bytes 6684672 | tf_op jit(solution)/shard_map/wlcma,wmco->lao/dot_general | solution.py:86
  254.9 9.7 %reshape.346 = f32[16,32,2,16,24]{4,3,2,1,0:T(8,128)} reshape(f32[16,24576]{1,0:T(8,128)} %reduce.4) | data formatting | bytes 3145728 | tf_op jit(solution)/shard_map/reshape | solution.py:85
  264.5 17.9 %bitcast_convert_fusion.1 = (bf16[32,24,768]{2,1,0:T(8,128)(2,1)}, f32[32,24,768,1,1]{2,1,3,0,4:T(8,128)}) fusion(f32[16,32,2,16,24]{4,3,2,1,0:T(8,128)} %reshape.346, f32[16,16,1,768]{3,1,2,0:T(8,128)} %get-tuple-element.18, f32[16,16,1,768]{3,1,2,0:T(8,128)S(1)} %get-tuple-element.17), kind=kOutput, calls=%fused_computation.65 | convolution fusion | flops 3624861696 | bytes 6684672 | tf_op jit(solution)/shard_map/wlcma,wmco->lao/dot_general | solution.py:86
  293.8 9.2 %reshape.347 = f32[16,32,2,16,24]{4,3,2,1,0:T(8,128)} reshape(f32[16,24576]{1,0:T(8,128)} %reduce.5) | data formatting | bytes 3145728 | tf_op jit(solution)/shard_map/reshape | solution.py:85
  303.0 17.9 %bitcast_convert_fusion = (bf16[32,24,768]{2,1,0:T(8,128)(2,1)}, f32[32,24,768,1,1]{2,1,3,0,4:T(8,128)}) fusion(f32[16,32,2,16,24]{4,3,2,1,0:T(8,128)} %reshape.347, f32[16,16,1,768]{3,1,2,0:T(8,128)} %get-tuple-element.18, f32[16,16,1,768]{3,1,2,0:T(8,128)S(1)} %get-tuple-element.17), kind=kOutput, calls=%fused_computation.64 | convolution fusion | flops 3624861696 | bytes 6684672 | tf_op jit(solution)/shard_map/wlcma,wmco->lao/dot_general | solution.py:86
  331.6 56.6 %all_to_all.94 = bf16[2,4,32,9216]{3,2,1,0:T(8,128)(2,1)S(1)} all-to-all(bf16[2,4,32,9216]{3,2,1,0:T(8,128)(2,1)S(1)} %pad_maximum_fusion), channel_id=1, replica_groups=mesh['wave'=16,'level'=2] {'level'}, dimensions={0} | all-to-all | bytes 9437184 | tf_op jit(solution)/shard_map/all_to_all | solution.py:91
  391.8 18.9 %fusion.7.clone.4 = bf16[1024,9216]{0,1:T(8,128)(2,1)} fusion(bf16[256,9216]{1,0:T(8,128)(2,1)S(1)} %fusion.24, bf16[1024,256]{1,0:T(8,128)(2,1)S(1)} %copy-done.19, f32[1024]{0:T(1024)S(1)} %copy-done.21), kind=kOutput, calls=%fused_computation.9.clone.clone.clone.1 | convolution fusion | flops 4926210048 | bytes 24121344 | tf_op jit(solution)/shard_map/dot_general | solution.py:37
  410.7 38.9 %fusion.15 = bf16[1024,9216]{0,1:T(8,128)(2,1)} fusion(bf16[1024,1024]{1,0:T(8,128)(2,1)S(1)} %copy-done, f32[1024]{0:T(1024)S(1)} %copy-done.22, bf16[1024,9216]{0,1:T(8,128)(2,1)} %fusion.7.clone.4), kind=kOutput, calls=%fused_computation.17 | convolution fusion | flops 19421724672 | bytes 39849984 | tf_op jit(solution)/shard_map/dot_general | solution.py:40
  449.6 19.2 %fusion.21 = bf16[9216,256]{0,1:T(8,128)(2,1)S(1)} fusion(bf16[1024,9216]{0,1:T(8,128)(2,1)} %fusion.15, bf16[256,1024]{1,0:T(8,128)(2,1)S(1)} %copy-done.20, f32[256]{0:T(256)S(1)} %copy-done.23), kind=kOutput, calls=%fused_computation.24 | convolution fusion | flops 4836556800 | bytes 24118272 | tf_op jit(solution)/shard_map/dot_general | solution.py:43
  483.9 49.8 %all-to-all-done.5 = bf16[4,64,9216]{2,0,1:T(4,128)(2,1)} async-done(((bf16[4,64,9216]{2,0,1:T(4,128)(2,1)}), bf16[4,64,9216]{2,0,1:T(4,128)(2,1)}, u32[]{:S(2)}, u32[]{:S(2)}) %all-to-all-start.5) | async-done | bytes 4718624 | tf_op jit(solution)/shard_map/all_to_all | solution.py:106
  538.6 8.2 copy.69
  546.7 13.1 %reshape.355 = f32[4,32,24,768]{3,2,1,0:T(8,128)} reshape(f32[4,32,2,9216]{3,2,1,0:T(2,128)} %copy.69) | data formatting | bytes 18874368 | tf_op jit(solution)/shard_map/convert_element_type | solution.py:109
  570.1 17.0 %convolution_bitcast_fusion.3 = f32[16,32,2,16,24]{1,3,4,2,0:T(8,128)} fusion(f32[32,24,768,1,1]{2,1,0,4,3:T(8,128)S(1)} %get-tuple-element.8, f32[768,16,16,1]{0,2,3,1:T(8,128)S(1)} %get-tuple-element.16, f32[768,16,16,1]{0,2,3,1:T(8,128)S(1)} %get-tuple-element.15), kind=kOutput, calls=%fused_computation.48 | convolution fusion | flops 3624665088 | bytes 5505024 | tf_op jit(solution)/shard_map/lao,owmc->wlcma/dot_general | solution.py:112
  587.1 10.9 %copy.75 = f32[16,32,2,16,24]{4,3,2,1,0:T(8,128)} copy(f32[16,32,2,16,24]{1,3,4,2,0:T(8,128)} %convolution_bitcast_fusion.3) | data formatting | bytes 3145728 | tf_op jit(solution)/shard_map/lao,owmc->wlcma/transpose | solution.py:112
  598.0 9.1 %all_to_all.81 = f32[16,1,24576]{2,1,0:T(1,128)} reshape(f32[16,32,2,16,24]{4,3,2,1,0:T(8,128)} %copy.75) | data formatting | bytes 3145728 | tf_op jit(solution)/shard_map/all_to_all | solution.py:115
  612.5 18.5 %convolution_bitcast_fusion.4 = f32[16,32,2,16,24]{1,3,4,2,0:T(8,128)} fusion(f32[32,24,768,1,1]{2,1,0,4,3:T(8,128)} %get-tuple-element.5, f32[768,16,16,1]{0,2,3,1:T(8,128)} %copy-done.9, f32[768,16,16,1]{0,2,3,1:T(8,128)S(1)} %get-tuple-element.15), kind=kOutput, calls=%fused_computation.49 | convolution fusion | flops 3624665088 | bytes 5505024 | tf_op jit(solution)/shard_map/lao,owmc->wlcma/dot_general | solution.py:112
  630.9 10.5 %copy.71 = f32[16,32,2,16,24]{4,3,2,1,0:T(8,128)} copy(f32[16,32,2,16,24]{1,3,4,2,0:T(8,128)} %convolution_bitcast_fusion.4) | data formatting | bytes 3145728 | tf_op jit(solution)/shard_map/lao,owmc->wlcma/transpose | solution.py:112
  641.4 9.1 %all_to_all.80 = f32[16,1,24576]{2,1,0:T(1,128)} reshape(f32[16,32,2,16,24]{4,3,2,1,0:T(8,128)} %copy.71) | data formatting | bytes 3145728 | tf_op jit(solution)/shard_map/all_to_all | solution.py:115
  657.9 18.5 %convolution_bitcast_fusion.2 = f32[16,32,2,16,24]{1,3,4,2,0:T(8,128)} fusion(f32[32,24,768,1,1]{2,1,0,4,3:T(8,128)} %get-tuple-element.7, f32[768,16,16,1]{0,2,3,1:T(8,128)} %copy-done.9, f32[768,16,16,1]{0,2,3,1:T(8,128)S(1)} %get-tuple-element.15), kind=kOutput, calls=%fused_computation.47 | convolution fusion | flops 3624665088 | bytes 5505024 | tf_op jit(solution)/shard_map/lao,owmc->wlcma/dot_general | solution.py:112
  676.3 10.5 %copy.80 = f32[16,32,2,16,24]{4,3,2,1,0:T(8,128)} copy(f32[16,32,2,16,24]{1,3,4,2,0:T(8,128)} %convolution_bitcast_fusion.2) | data formatting | bytes 3145728 | tf_op jit(solution)/shard_map/lao,owmc->wlcma/transpose | solution.py:112
  686.8 9.1 %all_to_all.82 = f32[16,1,24576]{2,1,0:T(1,128)} reshape(f32[16,32,2,16,24]{4,3,2,1,0:T(8,128)} %copy.80) | data formatting | bytes 3145728 | tf_op jit(solution)/shard_map/all_to_all | solution.py:115
  702.3 18.5 %convolution_bitcast_fusion.1 = f32[16,32,2,16,24]{1,3,4,2,0:T(8,128)} fusion(f32[32,24,768,1,1]{2,1,0,4,3:T(8,128)} %get-tuple-element.6, f32[768,16,16,1]{0,2,3,1:T(8,128)} %copy-done.9, f32[768,16,16,1]{0,2,3,1:T(8,128)S(1)} %get-tuple-element.15), kind=kOutput, calls=%fused_computation.46 | convolution fusion | flops 3624665088 | bytes 5505024 | tf_op jit(solution)/shard_map/lao,owmc->wlcma/dot_general | solution.py:112
  720.8 10.5 %copy.84 = f32[16,32,2,16,24]{4,3,2,1,0:T(8,128)} copy(f32[16,32,2,16,24]{1,3,4,2,0:T(8,128)} %convolution_bitcast_fusion.1) | data formatting | bytes 3145728 | tf_op jit(solution)/shard_map/lao,owmc->wlcma/transpose | solution.py:112
  731.3 9.1 %all_to_all.83 = f32[16,1,24576]{2,1,0:T(1,128)} reshape(f32[16,32,2,16,24]{4,3,2,1,0:T(8,128)} %copy.84) | data formatting | bytes 3145728 | tf_op jit(solution)/shard_map/all_to_all | solution.py:115
  752.2 8.5 reshape.350
  760.7 18.7 %fusion.42 = f32[32,16,2,256]{3,0,2,1:T(8,128)S(1)} fusion(f32[16,16,24,256,1]{3,2,1,4,0:T(8,128)} %bitcast.218, f32[16,32,2,16,24]{4,3,2,1,0:T(8,128)} %reshape.350), kind=kOutput, calls=%fused_computation.72 | convolution fusion | flops 1207959552 | bytes 8912896 | tf_op jit(solution)/shard_map/wlcma,mwaj->lmcj/dot_general | solution.py:119
  790.8 8.2 reshape.349
  804.2 8.1 reshape.352
  817.5 8.5 reshape.353
  826.0 18.6 %fusion.39 = f32[1,32,16,2,256]{4,1,3,2,0:T(8,128)S(1)} fusion(f32[16,16,24,256,1]{3,2,1,4,0:T(8,128)} %bitcast.219, f32[16,32,2,16,24]{4,3,2,1,0:T(8,128)} %reshape.349), kind=kOutput, calls=%fused_computation.71 | convolution fusion | flops 1207959552 | bytes 8912896 | tf_op jit(solution)/shard_map/wlcma,mwaj->lmcj/dot_general | solution.py:119
  844.7 19.8 %fusion.45 = f32[1,32,16,2,256]{4,1,3,2,0:T(8,128)} fusion(f32[16,16,24,256,1]{3,2,1,4,0:T(8,128)} %bitcast.220, f32[16,32,2,16,24]{4,3,2,1,0:T(8,128)} %reshape.352), kind=kOutput, calls=%fused_computation.73 | convolution fusion | flops 1207959552 | bytes 8912896 | tf_op jit(solution)/shard_map/wlcma,mwaj->lmcj/dot_general | solution.py:119
  864.6 19.7 %fusion.48 = f32[1,32,16,2,256]{4,1,3,2,0:T(8,128)} fusion(f32[16,16,24,256,1]{3,2,1,4,0:T(8,128)S(1)} %bitcast.223, f32[16,32,2,16,24]{4,3,2,1,0:T(8,128)S(1)} %bitcast.225), kind=kOutput, calls=%fused_computation.74 | convolution fusion | flops 1207959552 | bytes 8912896 | tf_op jit(solution)/shard_map/wlcma,mwaj->lmcj/dot_general | solution.py:119
  (126 shorter events, 188.3 us)
Async XLA Ops:
  6.5 404.2 %copy-start = (bf16[1024,1024]{1,0:T(8,128)(2,1)S(1)}, bf16[1024,1024]{1,0:T(8,128)(2,1)}, u32[]{:S(2)}) copy-start(bf16[1024,1024]{1,0:T(8,128)(2,1)} %param.22) | copy-start | bytes 6291460
  6.5 7.0 copy-start.3
  6.5 0.6 copy-start.13
  14.1 2.6 copy-start.2
  43.7 39.6 %all-to-all-start = ((f32[16,1,24576]{2,1,0:T(1,128)}), f32[16,1,24576]{2,1,0:T(1,128)}, u32[]{:S(2)}, u32[]{:S(2)}) async-start(f32[16,1,24576]{2,1,0:T(1,128)} %all_to_all.76), calls=%async_computation | async-start | bytes 3145728 | tf_op jit(solution)/shard_map/all_to_all | solution.py:82
  83.3 41.0 %all-to-all-start.1 = ((f32[16,1,24576]{2,1,0:T(1,128)}), f32[16,1,24576]{2,1,0:T(1,128)}, u32[]{:S(2)}, u32[]{:S(2)}) async-start(f32[16,1,24576]{2,1,0:T(1,128)} %all_to_all.77), calls=%async_computation.1 | async-start | bytes 3145728 | tf_op jit(solution)/shard_map/all_to_all | solution.py:82
  124.3 97.6 %all-to-all-start.2 = ((f32[16,1,24576]{2,1,0:T(1,128)}), f32[16,1,24576]{2,1,0:T(1,128)}, u32[]{:S(2)}, u32[]{:S(2)}) async-start(f32[16,1,24576]{2,1,0:T(1,128)} %all_to_all.78), calls=%async_computation.2 | async-start | bytes 3145728 | tf_op jit(solution)/shard_map/all_to_all | solution.py:82
  165.3 0.6 copy-start.10
  221.9 65.5 %all-to-all-start.3 = ((f32[16,1,24576]{2,1,0:T(1,128)}), f32[16,1,24576]{2,1,0:T(1,128)}, u32[]{:S(2)}, u32[]{:S(2)}) async-start(f32[16,1,24576]{2,1,0:T(1,128)} %all_to_all.79), calls=%async_computation.3 | async-start | bytes 3145728 | tf_op jit(solution)/shard_map/all_to_all | solution.py:82
  320.9 5.2 copy-start.6
  323.6 3.5 copy-start.7
  389.2 1.1 copy-start.15
  390.4 1.4 copy-start.19
  390.4 1.4 copy-start.21
  391.7 19.0 %copy-start.22 = (f32[1024]{0:T(1024)S(1)}, f32[1024]{0:T(1024)}, u32[]{:S(2)}) copy-start(f32[1024]{0:T(1024)} %param.23) | copy-start | bytes 12292
  410.7 38.9 %copy-start.20 = (bf16[256,1024]{1,0:T(8,128)(2,1)S(1)}, bf16[256,1024]{1,0:T(8,128)(2,1)}, u32[]{:S(2)}) copy-start(bf16[256,1024]{1,0:T(8,128)(2,1)} %param.24) | copy-start | bytes 1572868
  410.7 38.9 %copy-start.23 = (f32[256]{0:T(256)S(1)}, f32[256]{0:T(256)}, u32[]{:S(2)}) copy-start(f32[256]{0:T(256)} %param.25) | copy-start | bytes 3076
  474.7 5.9 copy-start.11
  474.7 59.0 %all-to-all-start.5 = ((bf16[4,64,9216]{2,0,1:T(4,128)(2,1)}), bf16[4,64,9216]{2,0,1:T(4,128)(2,1)}, u32[]{:S(2)}, u32[]{:S(2)}) async-start(bf16[4,64,9216]{2,0,1:T(4,128)(2,1)} %copy.67), calls=%async_computation.5 | async-start | bytes 9437184 | tf_op jit(solution)/shard_map/all_to_all | solution.py:106
  483.9 86.2 %copy-start.9 = (f32[768,16,16,1]{0,2,3,1:T(8,128)}, f32[768,16,16,1]{0,2,3,1:T(8,128)S(1)}, u32[]{:S(2)}) copy-start(f32[768,16,16,1]{0,2,3,1:T(8,128)S(1)} %get-tuple-element.16) | copy-start | bytes 2359300
  546.7 13.1 %copy-start.18 = (f32[24]{0:T(128)S(1)}, f32[24]{0:T(128)}, u32[]{:S(2)}) copy-start(f32[24]{0:T(128)} %param.15) | copy-start | bytes 292
  607.1 43.4 %all-to-all-start.7 = ((f32[16,1,24576]{2,1,0:T(1,128)}), f32[16,1,24576]{2,1,0:T(1,128)S(1)}, u32[]{:S(2)}, u32[]{:S(2)}) async-start(f32[16,1,24576]{2,1,0:T(1,128)} %all_to_all.81), calls=%async_computation.7 | async-start | bytes 3145728 | tf_op jit(solution)/shard_map/all_to_all | solution.py:115
  650.5 1.1 copy-start.5
  651.7 44.3 %all-to-all-start.6 = ((f32[16,1,24576]{2,1,0:T(1,128)}), f32[16,1,24576]{2,1,0:T(1,128)S(1)}, u32[]{:S(2)}, u32[]{:S(2)}) async-start(f32[16,1,24576]{2,1,0:T(1,128)} %all_to_all.80), calls=%async_computation.6 | async-start | bytes 3145728 | tf_op jit(solution)/shard_map/all_to_all | solution.py:115
  696.0 24.8 %copy-start.4 = (f32[16,1,24576]{2,1,0:T(1,128)}, f32[16,1,24576]{2,1,0:T(1,128)S(1)}, u32[]{:S(2)}) copy-start(f32[16,1,24576]{2,1,0:T(1,128)S(1)} %all-to-all-done.6) | copy-start | bytes 4718596
  696.0 44.5 %all-to-all-start.8 = ((f32[16,1,24576]{2,1,0:T(1,128)}), f32[16,1,24576]{2,1,0:T(1,128)}, u32[]{:S(2)}, u32[]{:S(2)}) async-start(f32[16,1,24576]{2,1,0:T(1,128)} %all_to_all.82), calls=%async_computation.8 | async-start | bytes 3145728 | tf_op jit(solution)/shard_map/all_to_all | solution.py:115
  731.3 15.4 %copy-start.14 = (s32[16]{0:T(128)S(1)}, s32[16]{0:T(128)}, u32[]{:S(2)}) copy-start(s32[16]{0:T(128)} %copy-done.13) | copy-start | bytes 196
  731.3 15.5 %copy-start.16 = (f32[64]{0:T(128)S(1)}, f32[64]{0:T(128)}, u32[]{:S(2)}) copy-start(f32[64]{0:T(128)} %param.17) | copy-start | bytes 772
  740.4 71.9 %all-to-all-start.9 = ((f32[16,1,24576]{2,1,0:T(1,128)}), f32[16,1,24576]{2,1,0:T(1,128)}, u32[]{:S(2)}, u32[]{:S(2)}) async-start(f32[16,1,24576]{2,1,0:T(1,128)} %all_to_all.83), calls=%async_computation.9 | async-start | bytes 3145728 | tf_op jit(solution)/shard_map/all_to_all | solution.py:115
  746.6 137.6 %all-gather.2.cloned.1.call-start = ((), (), s32[]{:S(2)}) async-start(), calls=%async_computation.10 | async-start | bytes 3145728 | tf_op jit(solution)/shard_map/all_gather | solution.py:129
  779.3 2.7 copy-start.17
  826.0 38.4 %slice-start = ((s8[6291456]{0:T(1024)(128)(4,1)}), s8[4194304]{0:T(1024)(128)(4,1)S(1)}, s32[]{:S(2)}) async-start(s8[6291456]{0:T(1024)(128)(4,1)} %bitcast.221), calls=%async_computation.11 | async-start | bytes 8388608
  826.0 38.5 %slice-start.2 = ((s8[8388608]{0:T(1024)(128)(4,1)}), s8[4194304]{0:T(1024)(128)(4,1)S(1)}, s32[]{:S(2)}) async-start(s8[8388608]{0:T(1024)(128)(4,1)} %bitcast.224), calls=%async_computation.13 | async-start | bytes 8388608
  844.7 19.8 %slice-start.1 = ((s8[6291456]{0:T(1024)(128)(4,1)}), s8[2097152]{0:T(1024)(128)(4,1)S(1)}, s32[]{:S(2)}) async-start(s8[6291456]{0:T(1024)(128)(4,1)} %bitcast.221), calls=%async_computation.12 | async-start | bytes 4194304
  844.7 19.8 %slice-start.3 = ((s8[8388608]{0:T(1024)(128)(4,1)}), s8[4194304]{0:T(1024)(128)(4,1)S(1)}, s32[]{:S(2)}) async-start(s8[8388608]{0:T(1024)(128)(4,1)} %bitcast.224), calls=%async_computation.14 | async-start | bytes 8388608
  864.5 19.7 %copy-start.8 = (f32[64,8192]{1,0:T(8,128)S(1)}, f32[64,8192]{1,0:T(8,128)}, u32[]{:S(2)}) copy-start(f32[64,8192]{1,0:T(8,128)} %reshape.351) | copy-start | bytes 6291460
  864.6 19.7 %copy-start.12 = (f32[64,64]{1,0:T(8,128)S(1)}, f32[64,64]{1,0:T(8,128)}, u32[]{:S(2)}) copy-start(f32[64,64]{1,0:T(8,128)} %param.16) | copy-start | bytes 49156
  890.5 7.9 copy-start.1
Sparse Core Ops, SparseCore 0:
  782.2 33.4 all-gather.1
